TPU v7x, 32 devices: a whole 2x2x4 slice. The times are simulated.
32 devices in a mesh: tx: 2 (over x), ty: 4 (over z), pg: 4 (over y, core).
Axes of the slice: x: 2, y: 2, z: 4, core: 2. Of those that a mesh axis runs over, the one named last changes fastest.
Arguments:
- direct_modes: bfloat16 [64, 3, 32, 512], P('pg', None, 'tx', 'ty'), may hold values from -6 to 6
- adjoint_modes: bfloat16 [64, 3, 32, 512], P(None, None, 'tx', 'ty'), may hold values from -6 to 6
- block_order: int32 [8], replicated, may hold values from 0 to 7, each once
Outputs:
- tensor: float32 [64, 64, 64], P('pg', 'ty', 'tx')
Inputs may be any that keep to these rules, and one draw needn't show every extreme that they name: `block_order`: each of the 8 blocks appears exactly once.
All inputs are finite; a program needn't handle non-finite values.
Results may differ from a plain program's by a relative error of at most 0.0043.
Values may be sent and summed in bfloat16 or wider, within the bound.
A program may use at most 64 MiB of HBM per device.

v0:
```python
import math
import jax
import jax.numpy as jnp
from jax import lax
from jax.sharding import PartitionSpec as P

NBLK = 8
JB = 4
CZ = 4


def extended(block, sides, width):
    for axis, dim in sides:
        count = lax.axis_size(axis)
        forward = [(i, i + 1) for i in range(count - 1)]
        backward = [(target, source) for source, target in forward]
        low = lax.ppermute(
            lax.slice_in_dim(block, block.shape[dim] - width, None, axis=dim), axis, forward
        )
        high = lax.ppermute(lax.slice_in_dim(block, 0, width, axis=dim), axis, backward)
        block = jnp.concatenate([low, block, high], axis=dim)
    return block


def depth_slope(values, depth):
    position = jnp.arange(values.shape[-1]) % depth
    upper = jnp.where(
        position == depth - 1, jnp.roll(values, depth - 1, -1), jnp.roll(values, -1, -1)
    )
    lower = jnp.where(position == 0, jnp.roll(values, 1 - depth, -1), jnp.roll(values, 1, -1))
    return (upper - lower) * 0.5


def slopes(values, wide_x, wide_y, depth):
    along_x = (wide_x[:, :, 2:] - wide_x[:, :, :-2]) * 0.5
    along_y = (wide_y[..., 2 * depth :] - wide_y[..., : -2 * depth]) * 0.5
    along_z = depth_slope(values, depth)
    return jnp.stack([along_x, along_y, along_z], 1).astype(jnp.bfloat16)


def pair_terms(rows_u, rows_g, cols_u, cols_g):
    result = jnp.zeros((rows_u.shape[0], cols_u.shape[0]) + cols_g.shape[2:], jnp.float32)
    for direction in range(3):
        result = result + rows_u[:, None, direction, None] * cols_g[None, :, direction]
        result = result + cols_u[None, :, direction, None] * rows_g[:, None, direction]
    return result.astype(jnp.bfloat16)


def project(pairs, adjoint):
    flat = pairs.reshape(pairs.shape[0] * pairs.shape[1], -1)
    basis = adjoint.reshape(adjoint.shape[0], -1)
    product = lax.dot_general(
        flat, basis, (((1,), (1,)), ((), ())), preferred_element_type=jnp.float32
    )
    return product.reshape(pairs.shape[0], pairs.shape[1], adjoint.shape[0])


def block_tensor(rows_u, rows_g, modes, grads, adjoint, width):
    count = modes.shape[0] // width

    def one_block(start):
        cols_u = lax.dynamic_slice_in_dim(modes, start, width, 0).astype(jnp.float32)
        cols_g = lax.dynamic_slice_in_dim(grads, start, width, 0).astype(jnp.float32)
        return project(pair_terms(rows_u, rows_g, cols_u, cols_g), adjoint)

    starts = jnp.arange(count) * width
    pieces = lax.map(one_block, starts)
    return jnp.transpose(pieces, (1, 0, 2, 3)).reshape(
        rows_u.shape[0], modes.shape[0], adjoint.shape[0]
    )


def shards(direct_modes, adjoint_modes, block_order):
    x_count = lax.axis_size("tx")
    y_count = lax.axis_size("ty")
    group_count = lax.axis_size("pg")
    weight = 1.0 / math.sqrt(
        3.0 * direct_modes.shape[2] * x_count * direct_modes.shape[3] * y_count
    )
    whole = lax.all_gather(direct_modes, "pg", axis=0, tiled=True)
    wide_x = extended(whole, (("tx", 2),), 1)
    wide_y = extended(whole, (("ty", 3),), CZ)
    grads = slopes(
        whole.astype(jnp.float32), wide_x.astype(jnp.float32), wide_y.astype(jnp.float32), CZ
    )
    mode_count = whole.shape[0]
    block_rows = mode_count // NBLK
    per_group = NBLK // group_count
    group_id = lax.axis_index("pg")
    mine = lax.dynamic_slice_in_dim(block_order, group_id * per_group, per_group, 0)
    row_index = (
        mine[:, None] * block_rows + jnp.arange(block_rows, dtype=jnp.int32)[None, :]
    ).reshape(-1)
    rows_u = jnp.take(whole, row_index, axis=0).astype(jnp.float32)
    rows_g = jnp.take(grads, row_index, axis=0).astype(jnp.float32)
    partial_sum = block_tensor(rows_u, rows_g, whole, grads, adjoint_modes, JB) * weight
    row_count = partial_sum.shape[0]
    j_width = mode_count // y_count
    k_width = adjoint_modes.shape[0] // x_count
    arranged = partial_sum.reshape(row_count, y_count, j_width, x_count, k_width)
    arranged = jnp.transpose(arranged, (0, 3, 1, 2, 4)).reshape(row_count, -1)
    shares = lax.psum_scatter(arranged, ("tx", "ty"), scatter_dimension=1, tiled=True)
    return shares.reshape(row_count, j_width, k_width)


def solution(mesh):
    placed = (P("pg", None, "tx", "ty"), P(None, None, "tx", "ty"), P())
    return jax.shard_map(
        shards, mesh=mesh, in_specs=placed, out_specs=P("pg", "ty", "tx"), check_vma=False
    )
```

profile of v0, /device:TPU:0, one launch (start us, length us, event | category | flops | bytes accessed | tf_op | source)
XLA Modules:
  0.0 225.4 jit_solution(8822786861770706708)
XLA Ops:
  6.5 10.3 %all_gather.3 = bf16[64,3,16,128]{3,2,1,0:T(8,128)(2,1)S(1)} all-gather(bf16[16,3,16,128]{3,2,1,0:T(8,128)(2,1)} %param.5), channel_id=1, replica_groups=mesh['tx'=2,'ty'=4,'pg'=4] {'pg'}, dimensions={0}, use_global_device_ids=true | all-gather | bytes 983040 | tf_op jit(solution)/shard_map/all_gather | solution.py:80
  17.1 1.3 copy.25
  18.4 4.1 %collective-permute-start.2 = (bf16[64,3,16,4]{0,2,3,1:T(8,128)(2,1)}, bf16[64,3,16,4]{0,2,3,1:T(8,128)(2,1)}, u32[]{:S(2)}, u32[]{:S(2)}) collective-permute-start(bf16[64,3,16,4]{0,2,3,1:T(8,128)(2,1)} %copy.25), channel_id=1, source_target_pairs={{0,4},{4,8},{8,12},{1,5},{5,9},{9,13},{2,6},{6,10},{10,14},{3,7},{... | collective-permute-start | bytes 73736 | tf_op jit(solution)/shard_map/ppermute | solution.py:17
  22.5 1.3 copy.26
  23.8 1.3 collective-permute-start.3
  25.9 4.0 %collective-permute-start = (bf16[64,3,1,128]{3,2,1,0:T(2,128)(2,1)}, bf16[64,3,1,128]{3,2,1,0:T(2,128)(2,1)}, u32[]{:S(2)}, u32[]{:S(2)}) collective-permute-start(bf16[64,3,1,128]{3,2,1,0:T(2,128)(2,1)} %get-tuple-element.106), channel_id=1, source_target_pairs={{0,16},{1,17},{2,18},{3,19},{4,20},{5,21},{6,22},{7,23},{8,24},{9,... | collective-permute-start | bytes 147464 | tf_op jit(solution)/shard_map/ppermute | solution.py:17
  30.0 1.5 collective-permute-start.1
  31.6 2.2 slice_bitcast_fusion.12
  33.7 2.1 slice_bitcast_fusion.14
  35.9 2.2 slice_bitcast_fusion.13
  38.1 1.5 fusion.28
  39.9 2.0 copy.29
  41.9 1.8 copy.30
  44.4 1.8 copy.32
  46.9 6.8 %fusion.21 = bf16[64,1,3,16,128]{4,3,2,1,0:T(8,128)(2,1)} fusion(f32[64,1,3,16,125]{4,3,2,0,1:T(8,128)} %get-tuple-element.103, f32[64,1,3,16,3]{4,3,2,0,1:T(8,128)} %get-tuple-element.105, f32[64,1,3,16,1]{4,3,2,0,1:T(8,128)S(1)} %copy-done, f32[64,1,3,16,127]{4,3,2,0,1:T(8,128)} %get-tuple-element.101, f32[64,1,3,16,3]{4,3,2,0,1:T(8,128)} %get-tuple-element.104, ...), kind=kLoop, calls=%fused_computation.52 | loop fusion | flops 3538944 | bytes 7078144 | tf_op jit(solution)/shard_map/convert.2
  53.8 1.1 copy.40
  54.9 1.5 copy.27
  56.4 1.5 copy.28
  59.3 1.6 maximum_convert_fusion.1
  62.3 1.6 gather_fusion.1
  63.9 1.2 select_convert_fusion
  66.2 82.4 %while.10 = (s32[]{:T(128)}, f32[16,16,4,64]{3,1,2,0:T(8,128)}, f32[16,3,16,128]{3,0,2,1:T(8,128)S(1)}, s32[16]{0:T(128)S(1)}, bf16[64,3,3,16,128]{4,3,2,1,0:T(8...) while((s32[]{:T(128)}, f32[16,16,4,64]{3,1,2,0:T(8,128)}, ...), condition=%wide.region_1.2_spmd, body=%wide.region_0.1_spmd.sunk | while | flops 55148548 | bytes 7307939 | solution.py:67
  68.8 0.9 copy_convert_fusion.5
  69.9 1.4 fusion.32
  73.9 0.9 copy_convert_fusion.5
  75.1 1.4 fusion.32
  79.0 0.9 copy_convert_fusion.5
  80.2 1.4 fusion.32
  84.2 0.9 copy_convert_fusion.5
  85.4 1.5 fusion.32
  90.5 1.5 fusion.32
  95.7 1.5 fusion.32
  100.8 1.5 fusion.32
  106.0 1.5 fusion.32
  111.1 1.5 fusion.32
  116.3 1.5 fusion.32
  121.4 1.5 fusion.32
  126.6 1.4 fusion.32
  130.5 0.9 copy_convert_fusion.5
  131.7 1.5 fusion.32
  136.8 1.5 fusion.32
  142.0 1.5 fusion.32
  146.0 0.9 copy_convert_fusion.5
  147.1 1.5 fusion.32
  148.6 1.1 multiply_bitcast_fusion
  150.9 1.2 reshape.222
  152.2 64.9 %reduce-scatter.2.cloned.1.call-done = f32[16,512]{1,0:T(8,128)} async-done(((f32[16,4096]{1,0:T(8,128)}), f32[16,512]{1,0:T(8,128)}) %reduce-scatter.2.cloned.1.call-update) | async-done | bytes 32784 | tf_op jit(solution)/shard_map/reduce_scatter | solution.py:102
  217.1 1.5 reshape.223
  (148 shorter events, 29.8 us)
Async XLA Ops:
  6.5 210.5 %reduce-scatter.2.cloned.1.call-start = ((), (), s32[]{:S(2)}) async-start(), calls=%async_computation.1 | async-start | bytes 294912 | tf_op jit(solution)/shard_map/reduce_scatter | solution.py:102
  18.4 36.5 %collective-permute-start.2 = (bf16[64,3,16,4]{0,2,3,1:T(8,128)(2,1)}, bf16[64,3,16,4]{0,2,3,1:T(8,128)(2,1)}, u32[]{:S(2)}, u32[]{:S(2)}) collective-permute-start(bf16[64,3,16,4]{0,2,3,1:T(8,128)(2,1)} %copy.25), channel_id=1, source_target_pairs={{0,4},{4,8},{8,12},{1,5},{5,9},{9,13},{2,6},{6,10},{10,14},{3,7},{... | collective-permute-start | bytes 73736 | tf_op jit(solution)/shard_map/ppermute | solution.py:17
  23.8 32.6 %collective-permute-start.3 = (bf16[64,3,16,4]{0,2,3,1:T(8,128)(2,1)}, bf16[64,3,16,4]{0,2,3,1:T(8,128)(2,1)}, u32[]{:S(2)}, u32[]{:S(2)}) collective-permute-start(bf16[64,3,16,4]{0,2,3,1:T(8,128)(2,1)} %copy.26), channel_id=1, source_target_pairs={{4,0},{8,4},{12,8},{5,1},{9,5},{13,9},{6,2},{10,6},{14,10},{7,3},{... | collective-permute-start | bytes 73736 | tf_op jit(solution)/shard_map/ppermute | solution.py:20
  25.9 33.3 %collective-permute-start = (bf16[64,3,1,128]{3,2,1,0:T(2,128)(2,1)}, bf16[64,3,1,128]{3,2,1,0:T(2,128)(2,1)}, u32[]{:S(2)}, u32[]{:S(2)}) collective-permute-start(bf16[64,3,1,128]{3,2,1,0:T(2,128)(2,1)} %get-tuple-element.106), channel_id=1, source_target_pairs={{0,16},{1,17},{2,18},{3,19},{4,20},{5,21},{6,22},{7,23},{8,24},{9,... | collective-permute-start | bytes 147464 | tf_op jit(solution)/shard_map/ppermute | solution.py:17
  30.0 29.3 %collective-permute-start.1 = (bf16[64,3,1,128]{3,2,1,0:T(2,128)(2,1)}, bf16[64,3,1,128]{3,2,1,0:T(2,128)(2,1)}, u32[]{:S(2)}, u32[]{:S(2)}) collective-permute-start(bf16[64,3,1,128]{3,2,1,0:T(2,128)(2,1)} %get-tuple-element.107), channel_id=1, source_target_pairs={{16,0},{17,1},{18,2},{19,3},{20,4},{21,5},{22,6},{23,7},{24,8},{25... | collective-permute-start | bytes 147464 | tf_op jit(solution)/shard_map/ppermute | solution.py:20
  38.1 1.5 copy-start.5
  44.4 2.5 %copy-start = (f32[64,1,3,16,1]{4,3,2,0,1:T(8,128)S(1)}, f32[64,1,3,16,1]{4,3,2,0,1:T(8,128)}, u32[]{:S(2)}) copy-start(f32[64,1,3,16,1]{4,3,2,0,1:T(8,128)} %copy.30) | copy-start | bytes 36868
  46.9 7.0 %copy-start.3 = (bf16[64,3,16,128]{3,2,1,0:T(8,128)(2,1)S(1)}, bf16[64,3,16,128]{3,2,1,0:T(8,128)(2,1)}, u32[]{:S(2)}) copy-start(bf16[64,3,16,128]{3,2,1,0:T(8,128)(2,1)} %param.6) | copy-start | bytes 2359300
  60.9 1.1 copy-start.2
  62.3 1.6 copy-start.1
  65.1 1.1 copy-start.4
Sparse Core Ops, SparseCore 0:
  152.3 64.7 reduce-scatter.1
where the time goes:
time: 227 us; the launch traced here: 225 us
  waiting for transfers between devices  64.9 us (29%)
  local copies, waits for them, and re-layouts  42.5 us (19%)
  loops' own time  31.8 us (14%)
  other arithmetic  28.2 us (12%)
  matrix products  23.3 us (10%)
  between operations  13.6 us (6%)
  starting transfers between devices  10.9 us (5%)
  blocking collectives  10.3 us (5%)
    reduce_scatter x1, waiting for transfers between devices, shards(): lax.psum_scatter(arranged, ('tx', 'ty'), scatter_dimension=1, tiled=True)  64.9 us
    another operation x1, loops' own time, block_tensor(): pieces = lax.map(one_block, starts)  31.8 us
    dot_general x16, matrix products, project(): lax.dot_general(flat, basis, (((1,), (1,)), ((), ())), preferred_element_...  23.3 us
    convert_element_type x16, other arithmetic, one_block(): lax.dynamic_slice_in_dim(grads, start, width, 0).astype(jnp.float32)  15 us
    all_gather x1, blocking collectives, shards(): whole = lax.all_gather(direct_modes, 'pg', axis=0, tiled=True)  10.3 us
    dynamic_slice x16, local copies, waits for them, and re-layouts, block_tensor(): pieces = lax.map(one_block, starts)  9.31 us
    ppermute x2, starting transfers between devices, extended(): lax.ppermute(lax.slice_in_dim(block, block.shape[dim] - width, None, axis...  8.12 us
    another operation x1, other arithmetic  6.81 us
  transfers between devices with their start and end apart: 5, of which 1 were waited for; matrix products, arithmetic and copies ran while one was open for 13% of the time, Pallas kernels for 0%

commit v1 on v0

--- a/solution.py
+++ b/solution.py
@@ -3,6 +3,7 @@
 import jax.numpy as jnp
 from jax import lax
 from jax.sharding import PartitionSpec as P
+from jax.lax import axis_index, axis_size, ppermute
 
 NBLK = 8
 JB = 4
@@ -77,7 +78,26 @@
     weight = 1.0 / math.sqrt(
         3.0 * direct_modes.shape[2] * x_count * direct_modes.shape[3] * y_count
     )
-    whole = lax.all_gather(direct_modes, "pg", axis=0, tiled=True)
+    out_arr, w_next, top = (axis_size("pg"), axis_index("pg"), direct_modes.shape[0])
+    fields = [no * out_arr if j == 0 else no for j, no in enumerate(direct_modes.shape)]
+    whole = lax.dynamic_update_slice_in_dim(
+        jnp.zeros(fields, direct_modes.dtype), direct_modes, w_next * top, axis=0
+    )
+    after = piece_out = direct_modes
+    kk = 1
+    while kk < out_arr // 2 + 1:
+        after = ppermute(
+            after, axis_name="pg", perm=[(j, (j + 1) % out_arr) for j in range(out_arr)]
+        )
+        whole = lax.dynamic_update_slice_in_dim(whole, after, (w_next - kk) % out_arr * top, axis=0)
+        if 2 * kk < out_arr:
+            piece_out = ppermute(
+                piece_out, axis_name="pg", perm=[(j, (j - 1) % out_arr) for j in range(out_arr)]
+            )
+            whole = lax.dynamic_update_slice_in_dim(
+                whole, piece_out, (w_next + kk) % out_arr * top, axis=0
+            )
+        kk = kk + 1
     wide_x = extended(whole, (("tx", 2),), 1)
     wide_y = extended(whole, (("ty", 3),), CZ)
     grads = slopes(

time: 227 us -> 221 us (0.974)
  blocking collectives: 10.3 us -> 0 us
  waiting for transfers between devices: 64.9 us -> 69.2 us
  starting transfers between devices: 10.9 us -> 15 us
  loops' own time: 31.8 us -> 28.3 us
    all_gather x1 -> x0, blocking collectives: 10.3 us -> none  [shards(): whole = lax.all_gather(direct_modes, 'pg', axis=0, tiled=True)]
    ppermute x0 -> x3, starting transfers between devices: none -> 4.47 us  [the longest x2 2.51 us: shards(): ppermute(after, axis_name='pg', perm=[(j, (j + 1) % out_arr) for j in ran...]
    another operation x1, loops' own time: 31.8 us -> 28.3 us  [block_tensor(): pieces = lax.map(one_block, starts)]
    ppermute x0 -> x3, waiting for transfers between devices: none -> 3.12 us  [the longest x2 3.12 us: shards(): ppermute(after, axis_name='pg', perm=[(j, (j + 1) % out_arr) for j in ran...]
  transfers between devices with their start and end apart: 5 -> 8, of which waited for: 1 -> 3; matrix products, arithmetic and copies ran while one was open for 13% -> 7% of each run, Pallas kernels for 0% -> 0%
where the time goes in v1:
time: 221 us; the launch traced here: 220 us
  waiting for transfers between devices  69.2 us (31%)
  local copies, waits for them, and re-layouts  42.5 us (19%)
  loops' own time  28.3 us (13%)
  other arithmetic  27.8 us (13%)
  matrix products  23.2 us (10%)
  starting transfers between devices  15 us (7%)
  between operations  13.7 us (6%)
    reduce_scatter x1, waiting for transfers between devices, shards(): lax.psum_scatter(arranged, ('tx', 'ty'), scatter_dimension=1, tiled=True)  66 us
    another operation x1, loops' own time, block_tensor(): pieces = lax.map(one_block, starts)  28.3 us
    dot_general x16, matrix products, project(): lax.dot_general(flat, basis, (((1,), (1,)), ((), ())), preferred_element_...  23.2 us
    convert_element_type x16, other arithmetic, one_block(): lax.dynamic_slice_in_dim(grads, start, width, 0).astype(jnp.float32)  15 us
    dynamic_slice x16, local copies, waits for them, and re-layouts, block_tensor(): pieces = lax.map(one_block, starts)  9.41 us
    ppermute x2, starting transfers between devices, extended(): lax.ppermute(lax.slice_in_dim(block, block.shape[dim] - width, None, axis...  7.82 us
    another operation x1, other arithmetic  6.76 us
  transfers between devices with their start and end apart: 8, of which 3 were waited for; matrix products, arithmetic and copies ran while one was open for 7% of the time, Pallas kernels for 0%

profile of v1, /device:TPU:0, one launch (start us, length us, event | category | flops | bytes accessed | tf_op | source)
XLA Modules:
  0.0 219.7 jit_solution(2281152613550214009)
XLA Ops:
  7.0 2.0 collective-permute-start.1
  9.9 2.3 %copy.43 = bf16[64,3,16,128]{3,0,2,1:T(8,128)(2,1)} copy(bf16[64,3,16,128]{3,2,1,0:T(8,128)(2,1)} %param.6) | data formatting | bytes 1572864 | tf_op jit(solution)/shard_map/while | solution.py:68
  12.6 2.1 collective-permute-start.2
  14.7 3.0 %collective-permute-done.2 = bf16[16,3,16,128]{3,2,1,0:T(8,128)(2,1)S(1)} collective-permute-done((bf16[16,3,16,128]{3,2,1,0:T(8,128)(2,1)S(1)}, bf16[16,3,16,128]{3,2,1,0:T(8,128)(2,1)S(1)}, u32[]{:S(2)}, u32[]{:S(2)}) %collective-permute-start.2) | collective-permute-done | bytes 196640 | tf_op jit(solution)/shard_map/ppermute | solution.py:89
  17.7 1.5 fusion.28
  19.3 2.2 slice_bitcast_fusion.12
  21.5 2.1 slice_bitcast_fusion.14
  23.6 2.2 %slice_bitcast_fusion.13 = (f32[64,1,3,16,3]{4,3,2,0,1:T(8,128)}, f32[64,1,3,16,3]{4,3,2,0,1:T(8,128)}) fusion(f32[64,3,16,128]{3,2,1,0:T(8,128)S(1)} %convert_element_type.31), kind=kLoop, calls=%fused_computation.36 | loop fusion | bytes 147456 | tf_op jit(solution)/shard_map/jit(_roll_static)/concatenate | solution.py:31
  25.8 1.2 fusion.27
  27.2 2.0 copy.31
  29.2 1.8 copy.32
  31.7 1.8 copy.34
  33.5 1.8 copy.27
  35.3 4.4 %collective-permute-start.5 = (bf16[64,3,16,4]{0,2,3,1:T(8,128)(2,1)S(1)}, bf16[64,3,16,4]{0,2,3,1:T(8,128)(2,1)S(1)}, u32[]{:S(2)}, u32[]{:S(2)}) collective-permute-start(bf16[64,3,16,4]{0,2,3,1:T(8,128)(2,1)S(1)} %copy.27), channel_id=1, source_target_pairs={{0,4},{4,8},{8,12},{1,5},{5,9},{9,13},{2,6},{6,10},{10,14},{3,7},{... | collective-permute-start | bytes 73736 | tf_op jit(solution)/shard_map/ppermute | solution.py:18
  40.4 1.3 collective-permute-start.6
  41.7 3.4 %collective-permute-start.3 = (bf16[64,3,1,128]{3,2,1,0:T(2,128)(2,1)S(1)}, bf16[64,3,1,128]{3,2,1,0:T(2,128)(2,1)S(1)}, u32[]{:S(2)}, u32[]{:S(2)}) collective-permute-start(bf16[64,3,1,128]{3,2,1,0:T(2,128)(2,1)S(1)} %get-tuple-element.106), channel_id=1, source_target_pairs={{0,16},{1,17},{2,18},{3,19},{4,20},{5,21},{6,22},{7,23},{8,24},{9,... | collective-permute-start | bytes 147464 | tf_op jit(solution)/shard_map/ppermute | solution.py:18
  45.1 1.5 collective-permute-start.4
  47.2 6.8 %fusion.21 = bf16[64,1,3,16,128]{4,3,2,1,0:T(8,128)(2,1)} fusion(f32[64,1,3,16,125]{4,3,2,0,1:T(8,128)} %get-tuple-element.103, f32[64,1,3,16,3]{4,3,2,0,1:T(8,128)} %get-tuple-element.105, f32[64,1,3,16,1]{4,3,2,0,1:T(8,128)S(1)} %copy-done, f32[64,1,3,16,127]{4,3,2,0,1:T(8,128)} %get-tuple-element.101, f32[64,1,3,16,3]{4,3,2,0,1:T(8,128)} %get-tuple-element.104, ...), kind=kLoop, calls=%fused_computation.52 | loop fusion | flops 3538944 | bytes 7078144 | tf_op jit(solution)/shard_map/convert.2
  58.9 1.6 gather_fusion.1
  60.5 1.2 select_convert_fusion
  62.8 78.9 %while.10 = (s32[]{:T(128)}, f32[16,16,4,64]{3,1,2,0:T(8,128)}, f32[16,3,16,128]{3,0,2,1:T(8,128)S(1)}, s32[16]{0:T(128)S(1)}, bf16[64,3,3,16,128]{4,3,2,1,0:T(8...) while((s32[]{:T(128)}, f32[16,16,4,64]{3,1,2,0:T(8,128)}, ...), condition=%wide.region_1.2_spmd, body=%wide.region_0.1_spmd.sunk | while | flops 55148548 | bytes 7307939 | solution.py:68
  65.2 0.9 copy_convert_fusion.5
  66.3 1.5 fusion.32
  70.1 0.9 copy_convert_fusion.5
  71.3 1.5 fusion.32
  75.0 0.9 copy_convert_fusion.5
  76.2 1.4 fusion.32
  80.0 0.9 copy_convert_fusion.5
  81.1 1.4 fusion.32
  84.9 0.9 copy_convert_fusion.5
  86.0 1.5 fusion.32
  89.8 0.9 copy_convert_fusion.5
  91.0 1.5 fusion.32
  94.7 0.9 copy_convert_fusion.5
  95.9 1.4 fusion.32
  100.8 1.5 fusion.32
  105.8 1.4 fusion.32
  110.7 1.4 fusion.32
  115.6 1.5 fusion.32
  120.6 1.5 fusion.32
  125.5 1.5 fusion.32
  130.4 1.4 fusion.32
  135.4 1.5 fusion.32
  140.3 1.5 fusion.32
  141.8 1.1 multiply_bitcast_fusion
  144.1 1.2 reshape.222
  145.3 66.0 %reduce-scatter.2.cloned.1.call-done = f32[16,512]{1,0:T(8,128)} async-done(((f32[16,4096]{1,0:T(8,128)}), f32[16,512]{1,0:T(8,128)}) %reduce-scatter.2.cloned.1.call-update) | async-done | bytes 32784 | tf_op jit(solution)/shard_map/reduce_scatter | solution.py:122
  211.3 1.5 reshape.223
  (156 shorter events, 32.1 us)
Async XLA Ops:
  6.5 5.8 %copy-start.4 = (bf16[16,3,16,128]{3,2,1,0:T(8,128)(2,1)S(1)}, bf16[16,3,16,128]{3,2,1,0:T(8,128)(2,1)}, u32[]{:S(2)}) copy-start(bf16[16,3,16,128]{3,2,1,0:T(8,128)(2,1)} %param.5) | copy-start | bytes 589828
  6.5 204.8 %reduce-scatter.2.cloned.1.call-start = ((), (), s32[]{:S(2)}) async-start(), calls=%async_computation.1 | async-start | bytes 294912 | tf_op jit(solution)/shard_map/reduce_scatter | solution.py:122
  6.5 6.0 %collective-permute-start = (bf16[16,3,16,128]{3,2,1,0:T(8,128)(2,1)}, bf16[16,3,16,128]{3,2,1,0:T(8,128)(2,1)S(1)}, u32[]{:S(2)}, u32[]{:S(2)}) collective-permute-start(bf16[16,3,16,128]{3,2,1,0:T(8,128)(2,1)} %param.5), channel_id=1, source_target_pairs={{0,1},{1,2},{2,3},{3,0},{4,5},{5,6},{6,7},{7,4},{8,9},{9,10},{10,1... | collective-permute-start | bytes 589832 | tf_op jit(solution)/shard_map/ppermute | solution.py:89
  7.0 7.7 %collective-permute-start.1 = (bf16[16,3,16,128]{3,2,1,0:T(8,128)(2,1)}, bf16[16,3,16,128]{3,2,1,0:T(8,128)(2,1)S(1)}, u32[]{:S(2)}, u32[]{:S(2)}) collective-permute-start(bf16[16,3,16,128]{3,2,1,0:T(8,128)(2,1)} %param.5), channel_id=1, source_target_pairs={{0,3},{1,0},{2,1},{3,2},{4,7},{5,4},{6,5},{7,6},{8,11},{9,8},{10,9... | collective-permute-start | bytes 589832 | tf_op jit(solution)/shard_map/ppermute | solution.py:94
  12.6 5.1 %collective-permute-start.2 = (bf16[16,3,16,128]{3,2,1,0:T(8,128)(2,1)S(1)}, bf16[16,3,16,128]{3,2,1,0:T(8,128)(2,1)S(1)}, u32[]{:S(2)}, u32[]{:S(2)}) collective-permute-start(bf16[16,3,16,128]{3,2,1,0:T(8,128)(2,1)S(1)} %collective-permute-done), channel_id=1, source_target_pairs={{0,1},{1,2},{2,3},{3,0},{4,5},{5,6},{6,7},{7,4},{8,9},{9,10},{10,1... | collective-permute-start | bytes 589832 | tf_op jit(solution)/shard_map/ppermute | solution.py:89
  31.7 15.5 %copy-start = (f32[64,1,3,16,1]{4,3,2,0,1:T(8,128)S(1)}, f32[64,1,3,16,1]{4,3,2,0,1:T(8,128)}, u32[]{:S(2)}) copy-start(f32[64,1,3,16,1]{4,3,2,0,1:T(8,128)} %copy.32) | copy-start | bytes 36868
  35.3 18.9 %collective-permute-start.5 = (bf16[64,3,16,4]{0,2,3,1:T(8,128)(2,1)S(1)}, bf16[64,3,16,4]{0,2,3,1:T(8,128)(2,1)S(1)}, u32[]{:S(2)}, u32[]{:S(2)}) collective-permute-start(bf16[64,3,16,4]{0,2,3,1:T(8,128)(2,1)S(1)} %copy.27), channel_id=1, source_target_pairs={{0,4},{4,8},{8,12},{1,5},{5,9},{9,13},{2,6},{6,10},{10,14},{3,7},{... | collective-permute-start | bytes 73736 | tf_op jit(solution)/shard_map/ppermute | solution.py:18
  40.4 14.5 %collective-permute-start.6 = (bf16[64,3,16,4]{0,2,3,1:T(8,128)(2,1)S(1)}, bf16[64,3,16,4]{0,2,3,1:T(8,128)(2,1)S(1)}, u32[]{:S(2)}, u32[]{:S(2)}) collective-permute-start(bf16[64,3,16,4]{0,2,3,1:T(8,128)(2,1)S(1)} %copy.28), channel_id=1, source_target_pairs={{4,0},{8,4},{12,8},{5,1},{9,5},{13,9},{6,2},{10,6},{14,10},{7,3},{... | collective-permute-start | bytes 73736 | tf_op jit(solution)/shard_map/ppermute | solution.py:21
  41.7 15.2 %collective-permute-start.3 = (bf16[64,3,1,128]{3,2,1,0:T(2,128)(2,1)S(1)}, bf16[64,3,1,128]{3,2,1,0:T(2,128)(2,1)S(1)}, u32[]{:S(2)}, u32[]{:S(2)}) collective-permute-start(bf16[64,3,1,128]{3,2,1,0:T(2,128)(2,1)S(1)} %get-tuple-element.106), channel_id=1, source_target_pairs={{0,16},{1,17},{2,18},{3,19},{4,20},{5,21},{6,22},{7,23},{8,24},{9,... | collective-permute-start | bytes 147464 | tf_op jit(solution)/shard_map/ppermute | solution.py:18
  45.1 11.8 %collective-permute-start.4 = (bf16[64,3,1,128]{3,2,1,0:T(2,128)(2,1)S(1)}, bf16[64,3,1,128]{3,2,1,0:T(2,128)(2,1)S(1)}, u32[]{:S(2)}, u32[]{:S(2)}) collective-permute-start(bf16[64,3,1,128]{3,2,1,0:T(2,128)(2,1)S(1)} %get-tuple-element.107), channel_id=1, source_target_pairs={{16,0},{17,1},{18,2},{19,3},{20,4},{21,5},{22,6},{23,7},{24,8},{25... | collective-permute-start | bytes 147464 | tf_op jit(solution)/shard_map/ppermute | solution.py:21
  57.5 1.1 copy-start.2
  58.9 1.6 copy-start.1
  61.7 1.1 copy-start.3
Sparse Core Ops, SparseCore 0:
  145.4 65.8 reduce-scatter.1
